TPU v7x, 32 devices: a whole 2x2x4 slice. The times are simulated.
32 devices in a mesh: seq: 8 (over y, x, core), mp: 4 (over z).
Axes of the slice: x: 2, y: 2, z: 4, core: 2. Of those that a mesh axis runs over, the one named last changes fastest.
Arguments:
- query_rows: bfloat16 [4096, 4096], P('seq', 'mp'), may hold values from -6 to 6
- key_rows: bfloat16 [4096, 4096], P('seq', 'mp'), may hold values from -6 to 6
- value_rows: bfloat16 [4096, 4096], P('seq', 'mp'), may hold values from -6 to 6
- cotangent: bfloat16 [4096, 4096], P('seq', 'mp'), may hold values from -6 to 6
- token_ids: int32 [4096], P('seq'), may hold values from 0 to 3
- class_weight: float32 [4], replicated, may hold values from 0.5 to 2
- output_weight: bfloat16 [4096, 4096], P('mp', 'seq'), may hold values from -0.09375 to 0.09375
- filter_taps: bfloat16 [256, 128], P('mp'), may hold values from -0.5 to 0.5
Outputs:
- grad_q: bfloat16 [4096, 4096], P('seq', 'mp')
- grad_k: bfloat16 [4096, 4096], P('seq', 'mp')
- grad_v: bfloat16 [4096, 4096], P('seq', 'mp')
- filter_grad: float32 [256, 128], P('mp')
All inputs are finite; a program needn't handle non-finite values.
Results may differ from a plain program's by a relative error of at most 0.0085.
Values may be sent and summed in bfloat16 or wider, within the bound.
A program may use at most 64 MiB of HBM per device.

v0:
```python
import functools
import math

import jax
import jax.numpy as jnp
from jax import lax
from jax.experimental import pallas as pl
from jax.experimental.pallas import tpu as pltpu
from jax.sharding import PartitionSpec as P


def passed_along(value, axis, steps):
    count = lax.axis_size(axis)
    initial, last = (max(0, -steps), min(count, count - steps))
    return lax.ppermute(value, axis, [(source, source + steps) for source in range(initial, last)])


def window_matrix(filter_rows):
    leading = filter_rows.shape[0]
    tap_count = filter_rows.shape[1]
    width = 2 * tap_count
    edge = jnp.zeros((leading, 1), filter_rows.dtype)
    tail = jnp.zeros((leading, tap_count), filter_rows.dtype)
    pattern = jnp.concatenate([edge, jnp.flip(filter_rows, axis=1), tail], axis=1)
    repeated = jnp.broadcast_to(pattern[:, None, :], (leading, tap_count, width + 1))
    flattened = repeated.reshape(leading, tap_count * (width + 1))[:, : tap_count * width]
    return flattened.reshape(leading, tap_count, width)


def lag_sums(gram_terms):
    leading = gram_terms.shape[0]
    tap_count = gram_terms.shape[1]
    flattened = gram_terms.reshape(leading, 2 * tap_count * tap_count)[:, 1:]
    padded = jnp.concatenate(
        [flattened, jnp.zeros((leading, tap_count + 1), gram_terms.dtype)], axis=1
    )
    skewed = padded.reshape(leading, tap_count, 2 * tap_count + 1)[:, :, :tap_count]
    return jnp.flip(jnp.sum(skewed, axis=1), axis=1)


def plain_shards(
    query_rows, key_rows, value_rows, cotangent, token_ids, class_weight, output_weight, filter_taps
):
    rows_here, chan_count = query_rows.shape
    tap_count = filter_taps.shape[1]
    groups_here = filter_taps.shape[0]
    group_size = chan_count // groups_here
    seq_count = lax.axis_size("seq")
    mixing = (key_rows.astype(jnp.float32) * value_rows.astype(jnp.float32)).astype(jnp.bfloat16)
    labels = lax.broadcasted_iota(jnp.int32, (1, class_weight.shape[0]), 1)
    picked = (token_ids[:, None] == labels).astype(jnp.float32)
    row_scale = jnp.dot(picked, class_weight, precision=lax.Precision.HIGHEST)
    weighted = (cotangent.astype(jnp.float32) * row_scale[:, None]).astype(jnp.bfloat16)
    weight_full = lax.all_gather(output_weight, "seq", axis=1, tiled=True)
    grad_y = lax.dot_general(
        lax.all_gather(weighted, "mp", axis=1, tiled=True),
        weight_full,
        (((1,), (1,)), ((), ())),
        preferred_element_type=jnp.float32,
    )
    grad_conv = (grad_y * query_rows.astype(jnp.float32)).astype(jnp.bfloat16)
    block_count = rows_here // tap_count
    toeplitz = window_matrix(filter_taps)
    earlier = passed_along(mixing[rows_here - tap_count :], "seq", 1)
    later_rows = passed_along(grad_conv[:tap_count], "seq", -1)
    extended = jnp.concatenate([earlier, mixing], axis=0).reshape(
        block_count + 1, tap_count, groups_here, group_size
    )
    window = jnp.concatenate([extended[:-1], extended[1:]], axis=1)
    conv_out = (
        jnp.einsum("gtu,bugk->btgk", toeplitz, window, preferred_element_type=jnp.float32)
        .reshape(rows_here, chan_count)
        .astype(jnp.bfloat16)
    )
    grad_ext = jnp.concatenate([grad_conv, later_rows], axis=0).reshape(
        block_count + 1, tap_count, groups_here, group_size
    )
    back_terms = jnp.einsum(
        "gtu,btgk->bugk", toeplitz, grad_ext, preferred_element_type=jnp.float32
    )
    grad_mixing = (
        (back_terms[:-1, tap_count:] + back_terms[1:, :tap_count])
        .reshape(rows_here, chan_count)
        .astype(jnp.bfloat16)
    )
    gram_terms = jnp.einsum(
        "btgk,bugk->gtu", grad_ext[:-1], window, preferred_element_type=jnp.float32
    )
    filter_term = lag_sums(gram_terms)
    summed = lax.psum(filter_term, "seq")
    factor = 1.0 / math.sqrt(group_size * rows_here * seq_count)
    filter_grad = summed * factor
    grad_q = (grad_y * conv_out.astype(jnp.float32)).astype(jnp.bfloat16)
    grad_k = (grad_mixing.astype(jnp.float32) * value_rows.astype(jnp.float32)).astype(jnp.bfloat16)
    grad_v = (grad_mixing.astype(jnp.float32) * key_rows.astype(jnp.float32)).astype(jnp.bfloat16)
    return (grad_q, grad_k, grad_v, filter_grad)


MESH = pl.DeviceIdType.MESH
PARTS = 4
NT = (((1,), (1,)), ((), ()))


def dot_nt(left, right):
    return lax.dot_general(left, right, NT, preferred_element_type=jnp.float32)


def mixer_kernel(
    group_size,
    cot_hbm, ids_ref, class_ref, w_ref, q_hbm, k_hbm, v_hbm, taps_ref,
    gq_hbm, gk_hbm, gv_hbm, fg_ref,
    cot_ref, q_ref, k_ref, v_ref, gq_ref, gk_ref, gv_ref,
    wt_all, w_all, acc, mext, gcext, conv, fwd_mat, bwd_mat, pats, sums, terms,
    wt_send, wt_recv, w_send, w_recv, halo_send, halo_recv, term_send, term_recv, local_sem, out_sem,
):
    rows, chans = q_ref.shape
    groups, taps = taps_ref.shape
    win = 2 * taps
    blocks = rows // taps
    lanes = 128
    per_tile = lanes // group_size
    tiles = chans // lanes
    stack = per_tile * taps
    feats = w_ref.shape[1]
    s = lax.axis_index("seq")
    z = lax.axis_index("mp")
    n_seq = 8
    core = s % 2
    x = (s // 2) % 2
    y = s // 4
    sx = s + 2 * (1 - 2 * x)
    sy = s + 4 * (1 - 2 * y)
    sd = sx + 4 * (1 - 2 * y)
    sc = s + 1 - 2 * core
    hi = z // 2
    blk1 = (1 - z) * (1 - hi) + (5 - z) * hi
    blk2 = 2 - hi
    blk3 = 3 - 3 * hi
    sgn = 3 - 2 * z
    end = (z % 3) == 0
    mid = (z % 3) != 0
    part_rows = rows // PARTS
    w_part = w_ref.shape[0] // PARTS

    barrier = pltpu.get_barrier_semaphore()
    for step in range(1, n_seq):
        pl.semaphore_signal(barrier, 1, device_id=((s + step) % n_seq, z), device_id_type=MESH)

    @pl.when(z > 0)
    def _():
        pl.semaphore_signal(barrier, 1, device_id=(s, z - 1), device_id_type=MESH)

    @pl.when(z < 3)
    def _():
        pl.semaphore_signal(barrier, 1, device_id=(s, z + 1), device_id_type=MESH)

    loads = [
        pltpu.make_async_copy(src, dst, local_sem.at[i])
        for i, (src, dst) in enumerate(
            ((cot_hbm, cot_ref), (k_hbm, k_ref), (v_hbm, v_ref), (q_hbm, q_ref), (w_ref, w_all.at[s]))
        )
    ]
    for load in loads:
        load.start()

    ids = ids_ref[...]
    scale = jnp.zeros(ids.shape, jnp.float32)
    for label in range(class_ref.shape[0]):
        scale = jnp.where(ids == label, class_ref[label], scale)
    scale = jnp.transpose(jnp.broadcast_to(scale, (lanes, rows)))
    loads[0].wait()
    for part in range(PARTS):
        span = pl.ds(part * part_rows, part_rows)
        for tile in range(cot_ref.shape[1] // lanes):
            cols = pl.ds(tile * lanes, lanes)
            wt_all[z, span, cols] = (
                cot_ref[span, cols].astype(jnp.float32)
                * scale[part * part_rows : (part + 1) * part_rows]
            ).astype(jnp.bfloat16)

    pl.semaphore_wait(barrier, n_seq + (z % 3 + 1) // 2)

    def wt_copy(src, way, blk, part, to_z):
        span = pl.ds(part * part_rows, part_rows)
        return pltpu.make_async_remote_copy(
            src_ref=wt_all.at[src, span],
            dst_ref=wt_all.at[blk, span],
            send_sem=wt_send.at[way, part],
            recv_sem=wt_recv.at[blk, part],
            device_id=(s, to_z),
            device_id_type=MESH,
        )

    def w_copy(src, slot, part, way, to_s):
        span = pl.ds(part * w_part, w_part)
        source = w_ref.at[span] if src is None else w_all.at[src, span]
        return pltpu.make_async_remote_copy(
            src_ref=source,
            dst_ref=w_all.at[slot, span],
            send_sem=w_send.at[way, part],
            recv_sem=w_recv.at[slot, part],
            device_id=(to_s, z),
            device_id_type=MESH,
        )

    for part in range(PARTS):
        w_copy(None, s, part, 0, sx).start()
        w_copy(None, s, part, 1, sy).start()
        w_copy(None, s, part, 2, sc).start()
    for part in range(PARTS):
        @pl.when(z < 3)
        def _():
            wt_copy(z, 0, z, part, z + 1).start()

        @pl.when(z > 0)
        def _():
            wt_copy(z, 1, z, part, z - 1).start()

    loads[1].wait()
    loads[2].wait()

    mext[pl.ds(rows + taps, taps // 2)] = jnp.zeros((taps // 2, chans), jnp.bfloat16)
    mext[pl.ds(taps, rows)] = (
        k_ref[...].astype(jnp.float32) * v_ref[...].astype(jnp.float32)
    ).astype(jnp.bfloat16)

    def forward_halo():
        return pltpu.make_async_remote_copy(
            src_ref=mext.at[pl.ds(rows, taps)],
            dst_ref=mext.at[pl.ds(0, taps)],
            send_sem=halo_send.at[0],
            recv_sem=halo_recv.at[0],
            device_id=((s + 1) % n_seq, z),
            device_id_type=MESH,
        )

    def backward_halo():
        return pltpu.make_async_remote_copy(
            src_ref=gcext.at[pl.ds(0, taps)],
            dst_ref=gcext.at[pl.ds(rows, taps)],
            send_sem=halo_send.at[1],
            recv_sem=halo_recv.at[1],
            device_id=((s + n_seq - 1) % n_seq, z),
            device_id_type=MESH,
        )

    tap_at = lax.broadcasted_iota(jnp.int32, (taps, win), 0)
    col_at = lax.broadcasted_iota(jnp.int32, (taps, win), 1)
    keep = (tap_at == col_at).astype(jnp.bfloat16)
    turn = (tap_at + col_at == taps).astype(jnp.bfloat16)
    pats[0] = jnp.dot(taps_ref[...], turn, preferred_element_type=jnp.float32)
    pats[1] = jnp.dot(taps_ref[...], keep, preferred_element_type=jnp.float32)

    def build(lo, hi_):
        @pl.loop(lo, hi_)
        def _(g):
            for which, out in ((0, fwd_mat), (1, bwd_mat)):
                row = jnp.broadcast_to(pats[which, pl.ds(g, 1), :], (taps, win))
                skew = pltpu.roll(row, 0, 1, stride=1, stride_axis=0)
                out[pl.ds(pl.multiple_of(g * taps, taps), taps), :] = skew.astype(jnp.bfloat16)

    lane_group = lax.broadcasted_iota(jnp.int32, (taps, win), 1) % lanes // group_size

    def window(ref, pair, cols):
        first = ref[pl.ds(2 * pair * taps, win), cols]
        second = ref[pl.ds((2 * pair + 1) * taps, win), cols]
        return jnp.concatenate([first, second], axis=1)

    def filtered(mat, ref, pair, tile, cols):
        res = jnp.dot(
            mat[pl.ds(pl.multiple_of(tile * stack, stack), stack), :],
            window(ref, pair, cols),
            preferred_element_type=jnp.float32,
        )
        out = res[:taps]
        for g in range(1, per_tile):
            out = jnp.where(lane_group == g, res[g * taps : (g + 1) * taps], out)
        return out

    def forward_pair(pair):
        @pl.loop(0, tiles, unroll=4)
        def _(tile):
            cols = pl.ds(pl.multiple_of(tile * lanes, lanes), lanes)
            out = filtered(fwd_mat, mext, pair, tile, cols).astype(jnp.bfloat16)
            conv[pl.ds(2 * pair * taps, taps), cols] = out[:, :lanes]
            conv[pl.ds((2 * pair + 1) * taps, taps), cols] = out[:, lanes:]

    def backward_pair(pair):
        @pl.loop(0, tiles, unroll=4)
        def _(tile):
            cols = pl.ds(pl.multiple_of(tile * lanes, lanes), lanes)
            out = filtered(bwd_mat, gcext, pair, tile, cols).astype(jnp.bfloat16)
            for half in range(2):
                span = pl.ds((2 * pair + half) * taps, taps)
                gm = out[:, half * lanes : (half + 1) * lanes].astype(jnp.float32)
                gk_ref[span, cols] = (gm * v_ref[span, cols].astype(jnp.float32)).astype(jnp.bfloat16)
                gv_ref[span, cols] = (gm * k_ref[span, cols].astype(jnp.float32)).astype(jnp.bfloat16)

    half = taps // 2

    def gram_part(part):
        @pl.loop(0, tiles, unroll=4)
        def _(tile):
            cols = pl.ds(pl.multiple_of(tile * lanes, lanes), lanes)
            rows_at = (part * taps, part * taps + half)
            near = jnp.concatenate([gcext[pl.ds(at, half), cols] for at in rows_at], axis=1)
            zero = jnp.zeros_like(near)
            left = jnp.concatenate(
                [jnp.where(lane_group[:half] == g, near, zero) for g in range(per_tile)], axis=0
            )
            right = jnp.concatenate([mext[pl.ds(at, win), cols] for at in rows_at], axis=1)
            res = dot_nt(left, right)
            for g in range(per_tile):
                total = res[g * half : g * half + 8]
                for a in range(1, half // 8):
                    piece = res[g * half + 8 * a : g * half + 8 * a + 8]
                    total = total + pltpu.roll(piece, win - 8 * a, 1)
                at = pl.ds(pl.multiple_of((tile * per_tile + g) * 8, 8), 8)
                if part == 0:
                    sums[at, :] = total
                else:
                    sums[at, :] += total

    def project(blk, row, count, first):
        @pl.loop(0, chans // 256, unroll=4)
        def _(n):
            cols = pl.ds(pl.multiple_of(n * 256, 256), 256)
            part = dot_nt(
                wt_all[blk, pl.ds(row, count), pl.ds(0, feats)], w_all[2 * blk, cols, :]
            ) + dot_nt(
                wt_all[blk, pl.ds(row, count), pl.ds(feats, feats)], w_all[2 * blk + 1, cols, :]
            )
            if first:
                acc[pl.ds(row, count), cols] = part
            else:
                acc[pl.ds(row, count), cols] += part

    def wait_wt(blk, part):
        wt_copy(z, 0, blk, part, z).wait_recv()

    def wait_w(slot, part):
        w_copy(None, slot, part, 0, s).wait_recv()

    @pl.when(s < n_seq - 1)
    def _():
        forward_halo().start()

    @pl.when(s == 0)
    def _():
        mext[pl.ds(0, taps)] = jnp.zeros((taps, chans), jnp.bfloat16)

    @pl.when(s == n_seq - 1)
    def _():
        gcext[pl.ds(rows, taps)] = jnp.zeros((taps, chans), jnp.bfloat16)

    quarter = groups // PARTS
    for part in range(PARTS):
        build(part * quarter, (part + 1) * quarter)
        wait_wt(blk1, part)

        @pl.when(mid)
        def _():
            wt_copy(blk1, 2, blk1, part, z + sgn).start()
            wait_wt(blk2, part)
            wt_copy(blk2, 3, blk2, part, z - sgn).start()

        wait_w(sx, part)
        w_copy(sx, sx, part, 3, sc).start()
        if part < PARTS // 2:
            w_copy(sx, sx, part, 4, sy).start()
        wait_w(sy, part)
        w_copy(sy, sy, part, 5, sc).start()
        if part >= PARTS // 2:
            w_copy(sy, sy, part, 4, sx).start()

    @pl.when(s > 0)
    def _():
        forward_halo().wait_recv()

    for part in range(PARTS):
        wait_w(sd, part)
        w_copy(sd, sd, part, 6, sc).start()
        if part == 0:
            forward_pair(0)
        if part == 2:
            forward_pair(1)
    for part in range(PARTS):
        for slot in (sc, sx + sc - s, sy + sc - s, sd + sc - s):
            wait_w(slot, part)
    loads[4].wait()

    def relay_last(part):
        @pl.when(mid)
        def _():
            wait_wt(blk3, part)
            wt_copy(blk3, 4, blk3, part, z - sgn).start()

    relay_last(0)
    relay_last(1)
    project(z, 0, rows, True)
    relay_last(2)
    project(blk1, 0, rows, False)
    relay_last(3)
    loads[3].wait()
    for part in range(PARTS):
        @pl.when(end)
        def _():
            wait_wt(blk2, part)

    project(blk2, 0, rows, False)

    def out_copy(which, part, count):
        span = pl.ds(part * part_rows, count * part_rows)
        src, dst = ((gq_ref, gq_hbm), (gk_ref, gk_hbm), (gv_ref, gv_hbm))[which]
        return pltpu.make_async_copy(src.at[span], dst.at[span], out_sem.at[which, part])

    for part in range(PARTS):
        @pl.when(end)
        def _():
            wait_wt(blk3, part)

        row = part * part_rows
        project(blk3, row, part_rows, False)
        span = pl.ds(row, part_rows)
        grad = acc[span]
        gcext[span] = (grad * q_ref[span].astype(jnp.float32)).astype(jnp.bfloat16)
        gq_ref[span] = (grad * conv[span].astype(jnp.float32)).astype(jnp.bfloat16)
        if part == 1:
            @pl.when(s > 0)
            def _():
                backward_halo().start()
        gram_part(part)
        out_copy(0, part, 1).start()
        if part == 2:
            backward_pair(0)

    slab = sums[...]
    sub = lax.broadcasted_iota(jnp.int32, slab.shape, 0) % 8
    for bit in (1, 2, 4):
        slab = jnp.where((sub // bit) % 2 == 1, pltpu.roll(slab, win - bit, 1), slab)
    own = jnp.sum(slab.reshape(groups, 8, win), axis=1)
    terms[s] = jnp.dot(
        own,
        (col_at.T + tap_at.T == taps).astype(jnp.float32),
        precision=lax.Precision.HIGHEST,
        preferred_element_type=jnp.float32,
    )
    for which in (1, 2):
        out_copy(which, 0, 2).start()

    @pl.when(s < n_seq - 1)
    def _():
        backward_halo().wait_recv()

    def term_copy(step):
        return pltpu.make_async_remote_copy(
            src_ref=terms.at[s],
            dst_ref=terms.at[s],
            send_sem=term_send.at[step],
            recv_sem=term_recv.at[s],
            device_id=((s + step) % n_seq, z),
            device_id_type=MESH,
        )

    for step in range(1, n_seq):
        term_copy(step).start()
    backward_pair(1)
    for which in (1, 2):
        out_copy(which, 2, 2).start()
    for step in range(1, n_seq):
        peer = (s + step) % n_seq
        pltpu.make_async_remote_copy(
            src_ref=terms.at[peer],
            dst_ref=terms.at[peer],
            send_sem=term_send.at[step],
            recv_sem=term_recv.at[peer],
            device_id=(peer, z),
            device_id_type=MESH,
        ).wait_recv()
    total = terms[0]
    for peer in range(1, n_seq):
        total = total + terms[peer]
    fg_ref[...] = total * (1.0 / math.sqrt(group_size * rows * n_seq))
    for part in range(PARTS):
        out_copy(0, part, 1).wait()
    for which in (1, 2):
        for part in (0, 2):
            out_copy(which, part, 2).wait()

    for part in range(PARTS):
        @pl.when(z < 3)
        def _():
            wt_copy(z, 0, z, part, z + 1).wait_send()

        @pl.when(z > 0)
        def _():
            wt_copy(z, 1, z, part, z - 1).wait_send()

        @pl.when(mid)
        def _():
            for way, blk in ((2, blk1), (3, blk2), (4, blk3)):
                wt_copy(blk, way, blk, part, z + sgn).wait_send()

        for way in range(7):
            w_copy(None, s, part, way, sc).wait_send()

    @pl.when(s < n_seq - 1)
    def _():
        forward_halo().wait_send()

    @pl.when(s > 0)
    def _():
        backward_halo().wait_send()

    for step in range(1, n_seq):
        term_copy(step).wait_send()


def fused_shards(
    query_rows, key_rows, value_rows, cotangent, token_ids, class_weight, output_weight, filter_taps
):
    rows, chans = query_rows.shape
    groups, taps = filter_taps.shape
    feats = output_weight.shape[1]
    group_size = chans // groups
    bf16, f32 = jnp.bfloat16, jnp.float32
    vmem = pl.BlockSpec(memory_space=pltpu.VMEM)
    anyspace = pl.BlockSpec(memory_space=pl.ANY)
    smem = pl.BlockSpec(memory_space=pltpu.SMEM)
    dma = pltpu.SemaphoreType.DMA
    return pl.pallas_call(
        functools.partial(mixer_kernel, group_size),
        out_shape=(
            jax.ShapeDtypeStruct((rows, chans), bf16),
            jax.ShapeDtypeStruct((rows, chans), bf16),
            jax.ShapeDtypeStruct((rows, chans), bf16),
            jax.ShapeDtypeStruct((groups, taps), f32),
        ),
        in_specs=[anyspace, vmem, smem, anyspace, anyspace, anyspace, anyspace, vmem],
        out_specs=(anyspace, anyspace, anyspace, vmem),
        scratch_shapes=[pltpu.VMEM((rows, chans), bf16) for _ in range(7)]
        + [
            pltpu.VMEM((4, rows, cotangent.shape[1]), bf16),
            pltpu.VMEM((8, chans, feats), bf16),
            pltpu.VMEM((rows, chans), f32),
            pltpu.VMEM((rows + taps + taps // 2, chans), bf16),
            pltpu.VMEM((rows + taps, chans), bf16),
            pltpu.VMEM((rows, chans), bf16),
            pltpu.VMEM((groups * taps, 2 * taps), bf16),
            pltpu.VMEM((groups * taps, 2 * taps), bf16),
            pltpu.VMEM((2, groups, 2 * taps), f32),
            pltpu.VMEM((groups * 8, 2 * taps), f32),
            pltpu.VMEM((8, groups, taps), f32),
            dma((5, PARTS)),
            dma((4, PARTS)),
            dma((7, PARTS)),
            dma((8, PARTS)),
            dma((2,)),
            dma((2,)),
            dma((8,)),
            dma((8,)),
            dma((5,)),
            dma((3, PARTS)),
        ],
        compiler_params=pltpu.CompilerParams(
            collective_id=0, has_side_effects=True, vmem_limit_bytes=60 * 2**20
        ),
        name="mixer",
    )(
        cotangent,
        token_ids.reshape(1, rows),
        class_weight,
        output_weight,
        query_rows,
        key_rows,
        value_rows,
        filter_taps,
    )


def solution(mesh):
    placed = (
        P("seq", "mp"),
        P("seq", "mp"),
        P("seq", "mp"),
        P("seq", "mp"),
        P("seq"),
        P(),
        P("mp", "seq"),
        P("mp", None),
    )
    fused = mesh.shape["seq"] == 8 and mesh.shape["mp"] == 4
    return jax.shard_map(
        fused_shards if fused else plain_shards,
        mesh=mesh,
        in_specs=placed,
        out_specs=(P("seq", "mp"), P("seq", "mp"), P("seq", "mp"), P("mp", None)),
        check_vma=False,
    )
```

profile of v0, /device:TPU:0, one launch (start us, length us, event | category | flops | bytes accessed | tf_op | source)
XLA Modules:
  0.0 89.6 jit_solution(4725164259867637801)
XLA Ops:
  0.6 83.4 %mixer.1 = (bf16[512,1024]{1,0:T(8,128)(2,1)}, bf16[512,1024]{1,0:T(8,128)(2,1)}, bf16[512,1024]{1,0:T(8,128)(2,1)}, f32[64,128]{1,0:T(8,128)}) custom-call(bf16[512,1024]{1,0:T(8,128)(2,1)} %cot_hbm.1, s32[1,512]{1,0:T(1,128)} %bitcast.1, f32[4]{0:T(128)} %class_ref.1, bf16[1024,512]{1,0:T(8,128)(2,1)} %w_ref.1, bf16[512,1024]{1,0:T(8,128)(2,1)} %q_hbm.1, ...), custom_call_target="tpu_custom_call" | custom-call | tf_op jit(solution)/shard_map/mixer/pallas_call | solution.py:531
  84.0 0.0 copy-start.1
  84.1 2.4 %copy.16 = bf16[512,1024]{1,0:T(8,128)(2,1)} copy(bf16[512,1024]{1,0:T(8,128)(2,1)} %get-tuple-element.8) | data formatting | bytes 2097152
  86.4 0.0 copy-done.1
  86.4 0.0 copy-start
  86.4 1.0 %copy.17 = bf16[512,1024]{1,0:T(8,128)(2,1)} copy(bf16[512,1024]{1,0:T(8,128)(2,1)S(1)} %copy-done.1) | data formatting | bytes 2097152
  87.4 0.6 copy-done
  88.0 0.0 copy-start.2
  88.0 1.0 %copy.18 = bf16[512,1024]{1,0:T(8,128)(2,1)} copy(bf16[512,1024]{1,0:T(8,128)(2,1)S(1)} %copy-done) | data formatting | bytes 2097152
  89.0 0.0 copy-done.2
  89.0 0.6 copy.19
Async XLA Ops:
  84.0 2.4 %copy-start.1 = (bf16[512,1024]{1,0:T(8,128)(2,1)S(1)}, bf16[512,1024]{1,0:T(8,128)(2,1)}, u32[]{:S(2)}) copy-start(bf16[512,1024]{1,0:T(8,128)(2,1)} %get-tuple-element.9) | copy-start | bytes 3145732
  86.4 1.6 %copy-start = (bf16[512,1024]{1,0:T(8,128)(2,1)S(1)}, bf16[512,1024]{1,0:T(8,128)(2,1)}, u32[]{:S(2)}) copy-start(bf16[512,1024]{1,0:T(8,128)(2,1)} %get-tuple-element.10) | copy-start | bytes 3145732
  88.0 1.0 %copy-start.2 = (f32[64,128]{1,0:T(8,128)S(1)}, f32[64,128]{1,0:T(8,128)}, u32[]{:S(2)}) copy-start(f32[64,128]{1,0:T(8,128)} %get-tuple-element.11) | copy-start | bytes 98308
where the time goes:
time: 89.8 us; the launch traced here: 89.6 us
  Pallas kernels  83.4 us (93%)
  local copies, waits for them, and re-layouts  5.55 us (6%)
    pallas_call x1, Pallas kernels, fused_shards(): pl.pallas_call(functools.partial(mixer_kernel, group_size), out_shape=(ja...  83.4 us
    unnamed x10, local copies, waits for them, and re-layouts  5.55 us

commit v1 on v0

--- a/solution.py
+++ b/solution.py
@@ -108,10 +108,10 @@
 def mixer_kernel(
     group_size,
     cot_hbm, ids_ref, class_ref, w_ref, q_hbm, k_hbm, v_hbm, taps_ref,
-    gq_hbm, gk_hbm, gv_hbm, fg_ref,
-    cot_ref, q_ref, k_ref, v_ref, gq_ref, gk_ref, gv_ref,
+    gq_ref, gk_ref, gv_ref, fg_ref,
+    cot_ref, q_ref, k_ref, v_ref,
     wt_all, w_all, acc, mext, gcext, conv, fwd_mat, bwd_mat, pats, sums, terms,
-    wt_send, wt_recv, w_send, w_recv, halo_send, halo_recv, term_send, term_recv, local_sem, out_sem,
+    wt_send, wt_recv, w_send, w_recv, halo_send, halo_recv, term_send, term_recv, local_sem,
 ):
     rows, chans = q_ref.shape
     groups, taps = taps_ref.shape
@@ -409,11 +409,6 @@
 
     project(blk2, 0, rows, False)
 
-    def out_copy(which, part, count):
-        span = pl.ds(part * part_rows, count * part_rows)
-        src, dst = ((gq_ref, gq_hbm), (gk_ref, gk_hbm), (gv_ref, gv_hbm))[which]
-        return pltpu.make_async_copy(src.at[span], dst.at[span], out_sem.at[which, part])
-
     for part in range(PARTS):
         @pl.when(end)
         def _():
@@ -430,7 +425,6 @@
             def _():
                 backward_halo().start()
         gram_part(part)
-        out_copy(0, part, 1).start()
         if part == 2:
             backward_pair(0)
 
@@ -445,8 +439,6 @@
         precision=lax.Precision.HIGHEST,
         preferred_element_type=jnp.float32,
     )
-    for which in (1, 2):
-        out_copy(which, 0, 2).start()
 
     @pl.when(s < n_seq - 1)
     def _():
@@ -465,8 +457,6 @@
     for step in range(1, n_seq):
         term_copy(step).start()
     backward_pair(1)
-    for which in (1, 2):
-        out_copy(which, 2, 2).start()
     for step in range(1, n_seq):
         peer = (s + step) % n_seq
         pltpu.make_async_remote_copy(
@@ -481,11 +471,6 @@
     for peer in range(1, n_seq):
         total = total + terms[peer]
     fg_ref[...] = total * (1.0 / math.sqrt(group_size * rows * n_seq))
-    for part in range(PARTS):
-        out_copy(0, part, 1).wait()
-    for which in (1, 2):
-        for part in (0, 2):
-            out_copy(which, part, 2).wait()
 
     for part in range(PARTS):
         @pl.when(z < 3)
@@ -514,6 +499,16 @@
 
     for step in range(1, n_seq):
         term_copy(step).wait_send()
+
+
+def store_kernel(*refs):
+    copies = [
+        pltpu.make_async_copy(refs[i], refs[4 + i], refs[8].at[i]) for i in range(4)
+    ]
+    for copy in copies:
+        copy.start()
+    for copy in copies:
+        copy.wait()
 
 
 def fused_shards(
@@ -528,17 +523,17 @@
     anyspace = pl.BlockSpec(memory_space=pl.ANY)
     smem = pl.BlockSpec(memory_space=pltpu.SMEM)
     dma = pltpu.SemaphoreType.DMA
-    return pl.pallas_call(
+    held = pl.pallas_call(
         functools.partial(mixer_kernel, group_size),
         out_shape=(
-            jax.ShapeDtypeStruct((rows, chans), bf16),
-            jax.ShapeDtypeStruct((rows, chans), bf16),
-            jax.ShapeDtypeStruct((rows, chans), bf16),
-            jax.ShapeDtypeStruct((groups, taps), f32),
+            pltpu.VMEM((rows, chans), bf16),
+            pltpu.VMEM((rows, chans), bf16),
+            pltpu.VMEM((rows, chans), bf16),
+            pltpu.VMEM((groups, taps), f32),
         ),
         in_specs=[anyspace, vmem, smem, anyspace, anyspace, anyspace, anyspace, vmem],
-        out_specs=(anyspace, anyspace, anyspace, vmem),
-        scratch_shapes=[pltpu.VMEM((rows, chans), bf16) for _ in range(7)]
+        out_specs=(vmem, vmem, vmem, vmem),
+        scratch_shapes=[pltpu.VMEM((rows, chans), bf16) for _ in range(4)]
         + [
             pltpu.VMEM((4, rows, cotangent.shape[1]), bf16),
             pltpu.VMEM((8, chans, feats), bf16),
@@ -560,7 +555,6 @@
             dma((8,)),
             dma((8,)),
             dma((5,)),
-            dma((3, PARTS)),
         ],
         compiler_params=pltpu.CompilerParams(
             collective_id=0, has_side_effects=True, vmem_limit_bytes=60 * 2**20
@@ -576,6 +570,15 @@
         value_rows,
         filter_taps,
     )
+    return pl.pallas_call(
+        store_kernel,
+        out_shape=tuple(jax.ShapeDtypeStruct(part.shape, part.dtype) for part in held),
+        in_specs=[vmem] * 4,
+        out_specs=(pl.BlockSpec(memory_space=pltpu.HBM),) * 4,
+        compiler_params=pltpu.CompilerParams(vmem_limit_bytes=56 * 2**20),
+        scratch_shapes=[dma((4,))],
+        name="store",
+    )(*(pltpu.with_memory_space_constraint(part, pltpu.VMEM) for part in held))
 
 
 def solution(mesh):

time: 89.8 us -> 85.2 us (0.949)
  local copies, waits for them, and re-layouts: 5.55 us -> 0 us
  Pallas kernels: 83.4 us -> 84.4 us
    unnamed x10 -> x0, local copies, waits for them, and re-layouts: 5.55 us -> none
    pallas_call x1 -> x2, Pallas kernels: 83.4 us -> 84.4 us  [the longest x1 82.7 us: fused_shards(): pl.pallas_call(functools.partial(mixer_kernel, group_size), out_shape=(pl...]
where the time goes in v1:
time: 85.2 us; the launch traced here: 85 us
  Pallas kernels  84.4 us (99%)
    pallas_call x1, Pallas kernels, fused_shards(): pl.pallas_call(functools.partial(mixer_kernel, group_size), out_shape=(pl...  82.7 us

profile of v1, /device:TPU:0, one launch (start us, length us, event | category | flops | bytes accessed | tf_op | source)
XLA Modules:
  0.0 85.0 jit_solution(9348830166319142230)
XLA Ops:
  0.6 82.7 %mixer.1 = (bf16[512,1024]{1,0:T(8,128)(2,1)S(1)}, bf16[512,1024]{1,0:T(8,128)(2,1)S(1)}, bf16[512,1024]{1,0:T(8,128)(2,1)S(1)}, f32[64,128]{1,0:T(8,128)S(1)}) custom-call(bf16[512,1024]{1,0:T(8,128)(2,1)} %cot_hbm.1, s32[1,512]{1,0:T(1,128)} %bitcast.1, f32[4]{0:T(128)} %class_ref.1, bf16[1024,512]{1,0:T(8,128)(2,1)} %w_ref.1, bf16[512,1024]{1,0:T(8,128)(2,1)} %q_hbm.1, ...), custom_call_target="tpu_custom_call" | custom-call | tf_op jit(solution)/shard_map/mixer/pallas_call | solution.py:526
  83.3 1.7 %store.1 = (bf16[512,1024]{1,0:T(8,128)(2,1)}, bf16[512,1024]{1,0:T(8,128)(2,1)}, bf16[512,1024]{1,0:T(8,128)(2,1)}, f32[64,128]{1,0:T(8,128)}) custom-call(bf16[512,1024]{1,0:T(8,128)(2,1)S(1)} %get-tuple-element.8.refs_0_, bf16[512,1024]{1,0:T(8,128)(2,1)S(1)} %get-tuple-element.9.refs_1_, bf16[512,1024]{1,0:T(8,128)(2,1)S(1)} %get-tuple-element.10.refs_2_, ...), custom_call_target="tpu_custom_call" | custom-call | tf_op jit(solution)/shard_map/store/pallas_call | solution.py:573

commit v2 on v1

--- a/solution.py
+++ b/solution.py
@@ -110,8 +110,8 @@
     cot_hbm, ids_ref, class_ref, w_ref, q_hbm, k_hbm, v_hbm, taps_ref,
     gq_ref, gk_ref, gv_ref, fg_ref,
     cot_ref, q_ref, k_ref, v_ref,
-    wt_all, w_all, acc, mext, gcext, conv, fwd_mat, bwd_mat, pats, sums, terms,
-    wt_send, wt_recv, w_send, w_recv, halo_send, halo_recv, term_send, term_recv, local_sem,
+    wt_all, w_all, x_all, p_all, acc, mext, gcext, conv, fwd_mat, bwd_mat, pats, sums, terms,
+    wt_send, wt_recv, w_send, w_recv, x_send, x_recv, p_send, p_recv, halo_send, halo_recv, term_send, term_recv, local_sem,
 ):
     rows, chans = q_ref.shape
     groups, taps = taps_ref.shape
@@ -133,14 +133,19 @@
     sd = sx + 4 * (1 - 2 * y)
     sc = s + 1 - 2 * core
     hi = z // 2
-    blk1 = (1 - z) * (1 - hi) + (5 - z) * hi
-    blk2 = 2 - hi
-    blk3 = 3 - 3 * hi
-    sgn = 3 - 2 * z
+    step_in = 1 - 2 * hi
+    near = z + 1 - 2 * (z % 2)
+    far_mid = 2 - hi
+    far_end = 3 - 3 * hi
     end = (z % 3) == 0
     mid = (z % 3) != 0
+    own_row = y == hi
+    end_near = jnp.logical_and(end, own_row)
+    end_far = jnp.logical_and(end, y != hi)
     part_rows = rows // PARTS
     w_part = w_ref.shape[0] // PARTS
+    x_part = x_all.shape[1] // PARTS
+    other = (sc, sx + sc - s, sy + sc - s, sd + sc - s)
 
     barrier = pltpu.get_barrier_semaphore()
     for step in range(1, n_seq):
@@ -203,18 +208,68 @@
             device_id_type=MESH,
         )
 
-    for part in range(PARTS):
-        w_copy(None, s, part, 0, sx).start()
-        w_copy(None, s, part, 1, sy).start()
-        w_copy(None, s, part, 2, sc).start()
-    for part in range(PARTS):
-        @pl.when(z < 3)
-        def _():
-            wt_copy(z, 0, z, part, z + 1).start()
-
-        @pl.when(z > 0)
-        def _():
-            wt_copy(z, 1, z, part, z - 1).start()
+    def x_copy(src, slot, part, way, to_s, to_z):
+        span = pl.ds(part * x_part, x_part)
+        if src is None:
+            source = w_ref.at[pl.ds(way * x_all.shape[1] + part * x_part, x_part)]
+        else:
+            source = x_all.at[src, span]
+        return pltpu.make_async_remote_copy(
+            src_ref=source,
+            dst_ref=x_all.at[slot, span],
+            send_sem=x_send.at[way, part],
+            recv_sem=x_recv.at[slot, part],
+            device_id=(to_s, to_z),
+            device_id_type=MESH,
+        )
+
+    def p_copy(part):
+        span = pl.ds(part * part_rows, part_rows)
+        return pltpu.make_async_remote_copy(
+            src_ref=p_all.at[span],
+            dst_ref=p_all.at[span],
+            send_sem=p_send.at[part],
+            recv_sem=p_recv.at[part],
+            device_id=(s, near),
+            device_id_type=MESH,
+        )
+
+    def wait_wt(blk, part):
+        wt_copy(z, 0, blk, part, near).wait_recv()
+
+    def wait_w(slot, part):
+        w_copy(slot, slot, part, 0, sc).wait_recv()
+
+    def wait_x(slot, part):
+        x_copy(slot, slot, part, 0, sc, z).wait_recv()
+
+    @pl.when(mid)
+    def _():
+        for part in range(PARTS):
+            wt_copy(z, 0, z, part, near).start()
+            wt_copy(z, 1, z, part, z + step_in).start()
+        for part in range(PARTS):
+            if part < PARTS // 2:
+                w_copy(None, s, part, 0, sx).start()
+                w_copy(None, s, part, 1, sy).start()
+            w_copy(None, s, part, 2, sc).start()
+
+    @pl.when(end_far)
+    def _():
+        for part in range(PARTS):
+            x_copy(None, s, part, 0, s, near).start()
+            x_copy(None, sy, part, 1, sy, z).start()
+
+    @pl.when(end_near)
+    def _():
+        for part in range(PARTS):
+            w_copy(None, s, part, 0, sx).start()
+            w_copy(None, s, part, 1, sy).start()
+            w_copy(None, s, part, 2, sc).start()
+
+    @pl.when(end)
+    def _():
+        wt_copy(z, 0, z, 0, near).start()
 
     loads[1].wait()
     loads[2].wait()
@@ -335,11 +390,19 @@
             else:
                 acc[pl.ds(row, count), cols] += part
 
-    def wait_wt(blk, part):
-        wt_copy(z, 0, blk, part, z).wait_recv()
-
-    def wait_w(slot, part):
-        w_copy(None, slot, part, 0, s).wait_recv()
+    def partial_part(part):
+        span = pl.ds(part * part_rows, part_rows)
+        for n in range(chans // 256):
+            base = 4 * hi if n * 256 >= x_all.shape[1] else 4 * (1 - hi)
+            block = pl.ds(n * 256 % x_all.shape[1], 256)
+            total = None
+            for i in range(4):
+                term = dot_nt(
+                    wt_all[2 * (1 - hi) + i // 2, span, pl.ds(i % 2 * feats, feats)],
+                    x_all[base + i, block, :],
+                )
+                total = term if total is None else total + term
+            p_all[span, pl.ds(n * 256, 256)] = total.astype(jnp.bfloat16)
 
     @pl.when(s < n_seq - 1)
     def _():
@@ -354,16 +417,32 @@
         gcext[pl.ds(rows, taps)] = jnp.zeros((taps, chans), jnp.bfloat16)
 
     quarter = groups // PARTS
-    for part in range(PARTS):
-        build(part * quarter, (part + 1) * quarter)
-        wait_wt(blk1, part)
-
-        @pl.when(mid)
-        def _():
-            wt_copy(blk1, 2, blk1, part, z + sgn).start()
-            wait_wt(blk2, part)
-            wt_copy(blk2, 3, blk2, part, z - sgn).start()
-
+    build(0, quarter)
+
+    @pl.when(mid)
+    def _():
+        for part in range(PARTS):
+            wait_x(s, part)
+            x_copy(s, s, part, 0, sx, z).start()
+            x_copy(s, s, part, 1, sy, z).start()
+            x_copy(s, s, part, 2, sc, z).start()
+        w_copy(None, s, 2, 0, sx).start()
+        w_copy(None, s, 2, 1, sy).start()
+
+    @pl.when(end_near)
+    def _():
+        for part in range(PARTS):
+            wait_x(s, part)
+            x_copy(s, s, part, 0, s, near).start()
+
+    @pl.when(end)
+    def _():
+        for part in range(1, PARTS):
+            wt_copy(z, 0, z, part, near).start()
+
+    build(quarter, 2 * quarter)
+
+    def relay_w(part):
         wait_w(sx, part)
         w_copy(sx, sx, part, 3, sc).start()
         if part < PARTS // 2:
@@ -373,50 +452,130 @@
         if part >= PARTS // 2:
             w_copy(sy, sy, part, 4, sx).start()
 
-    @pl.when(s > 0)
-    def _():
-        forward_halo().wait_recv()
-
-    for part in range(PARTS):
+    def relay_diagonal(part):
         wait_w(sd, part)
         w_copy(sd, sd, part, 6, sc).start()
-        if part == 0:
-            forward_pair(0)
-        if part == 2:
-            forward_pair(1)
+
+    def relay_wt(part):
+        wait_wt(near, part)
+        wt_copy(near, 2, near, part, z + step_in).start()
+
+    @pl.when(mid)
+    def _():
+        for part in range(PARTS):
+            wait_x(sx, part)
+            x_copy(sx, sx, part, 3, sc, z).start()
+            if part < PARTS // 2:
+                x_copy(sx, sx, part, 4, sy, z).start()
+            wait_x(sy, part)
+            x_copy(sy, sy, part, 5, sc, z).start()
+            if part >= PARTS // 2:
+                x_copy(sy, sy, part, 4, sx, z).start()
+        w_copy(None, s, 3, 0, sx).start()
+        w_copy(None, s, 3, 1, sy).start()
+        relay_wt(0)
+        relay_w(0)
+        relay_w(1)
+
+    @pl.when(end_near)
+    def _():
+        for part in range(PARTS):
+            wait_w(sx, part)
+            w_copy(sx, sx, part, 3, sc).start()
+            if part < PARTS // 2:
+                w_copy(sx, sx, part, 4, sy).start()
+
+    @pl.when(end_far)
+    def _():
+        for part in range(PARTS):
+            wait_w(sy, part)
+            w_copy(sy, sy, part, 5, sc).start()
+            if part >= PARTS // 2:
+                w_copy(sy, sy, part, 4, sx).start()
+        for part in range(PARTS):
+            relay_diagonal(part)
+
+    build(2 * quarter, groups)
+
+    @pl.when(mid)
+    def _():
+        relay_wt(1)
+        for part in range(PARTS):
+            wait_x(sd, part)
+            x_copy(sd, sd, part, 6, sc, z).start()
+        relay_w(2)
+        relay_wt(2)
+        relay_w(3)
+        for part in range(PARTS):
+            for slot in other:
+                wait_x(slot, part)
+            wait_wt(far_mid, part)
+        for part in range(2):
+            wait_wt(far_end, part)
+            partial_part(part)
+            p_copy(part).start()
+        relay_wt(3)
+
+    @pl.when(s > 0)
+    def _():
+        forward_halo().wait_recv()
+
+    forward_pair(0)
+    forward_pair(1)
+
+    @pl.when(mid)
+    def _():
+        relay_diagonal(0)
+        relay_diagonal(2)
+        wait_wt(far_end, 2)
+        partial_part(2)
+        p_copy(2).start()
+        relay_diagonal(1)
+        relay_diagonal(3)
+        wait_wt(far_end, 3)
+        partial_part(3)
+        p_copy(3).start()
+        for part in range(PARTS):
+            for slot in other:
+                wait_w(slot, part)
+
+    @pl.when(end_near)
+    def _():
+        for part in range(PARTS):
+            for slot in other[:2]:
+                wait_w(slot, part)
+
+    @pl.when(end_far)
+    def _():
+        for part in range(PARTS):
+            for slot in other[2:]:
+                wait_w(slot, part)
+
+    loads[4].wait()
+    project(z, 0, rows, True)
+
+    @pl.when(end)
+    def _():
+        for part in range(PARTS):
+            wait_wt(near, part)
+
+    project(near, 0, rows, False)
+
+    @pl.when(mid)
+    def _():
+        project(far_mid, 0, rows, False)
+        project(far_end, 0, rows, False)
+
+    loads[3].wait()
+
     for part in range(PARTS):
-        for slot in (sc, sx + sc - s, sy + sc - s, sd + sc - s):
-            wait_w(slot, part)
-    loads[4].wait()
-
-    def relay_last(part):
-        @pl.when(mid)
-        def _():
-            wait_wt(blk3, part)
-            wt_copy(blk3, 4, blk3, part, z - sgn).start()
-
-    relay_last(0)
-    relay_last(1)
-    project(z, 0, rows, True)
-    relay_last(2)
-    project(blk1, 0, rows, False)
-    relay_last(3)
-    loads[3].wait()
-    for part in range(PARTS):
+        span = pl.ds(part * part_rows, part_rows)
+
         @pl.when(end)
         def _():
-            wait_wt(blk2, part)
-
-    project(blk2, 0, rows, False)
-
-    for part in range(PARTS):
-        @pl.when(end)
-        def _():
-            wait_wt(blk3, part)
-
-        row = part * part_rows
-        project(blk3, row, part_rows, False)
-        span = pl.ds(row, part_rows)
+            p_copy(part).wait_recv()
+            acc[span] += p_all[span].astype(jnp.float32)
+
         grad = acc[span]
         gcext[span] = (grad * q_ref[span].astype(jnp.float32)).astype(jnp.bfloat16)
         gq_ref[span] = (grad * conv[span].astype(jnp.float32)).astype(jnp.bfloat16)
@@ -473,21 +632,29 @@
     fg_ref[...] = total * (1.0 / math.sqrt(group_size * rows * n_seq))
 
     for part in range(PARTS):
-        @pl.when(z < 3)
-        def _():
-            wt_copy(z, 0, z, part, z + 1).wait_send()
-
-        @pl.when(z > 0)
-        def _():
-            wt_copy(z, 1, z, part, z - 1).wait_send()
+        wt_copy(z, 0, z, part, near).wait_send()
 
         @pl.when(mid)
         def _():
-            for way, blk in ((2, blk1), (3, blk2), (4, blk3)):
-                wt_copy(blk, way, blk, part, z + sgn).wait_send()
-
-        for way in range(7):
-            w_copy(None, s, part, way, sc).wait_send()
+            wt_copy(z, 1, z, part, z + step_in).wait_send()
+            wt_copy(near, 2, near, part, z + step_in).wait_send()
+            p_copy(part).wait_send()
+            for way in range(7):
+                w_copy(s, s, part, way, sc).wait_send()
+                x_copy(s, s, part, way, sc, z).wait_send()
+
+        @pl.when(end_near)
+        def _():
+            x_copy(s, s, part, 0, s, near).wait_send()
+            for way in (0, 1, 2, 3) + ((4,) if part < PARTS // 2 else ()):
+                w_copy(s, s, part, way, sc).wait_send()
+
+        @pl.when(end_far)
+        def _():
+            for way in (0, 1):
+                x_copy(s, s, part, way, sy, z).wait_send()
+            for way in (5, 6) + ((4,) if part >= PARTS // 2 else ()):
+                w_copy(s, s, part, way, sc).wait_send()
 
     @pl.when(s < n_seq - 1)
     def _():
@@ -537,6 +704,8 @@
         + [
             pltpu.VMEM((4, rows, cotangent.shape[1]), bf16),
             pltpu.VMEM((8, chans, feats), bf16),
+            pltpu.VMEM((8, chans // 2, feats), bf16),
+            pltpu.VMEM((rows, chans), bf16),
             pltpu.VMEM((rows, chans), f32),
             pltpu.VMEM((rows + taps + taps // 2, chans), bf16),
             pltpu.VMEM((rows + taps, chans), bf16),
@@ -546,10 +715,14 @@
             pltpu.VMEM((2, groups, 2 * taps), f32),
             pltpu.VMEM((groups * 8, 2 * taps), f32),
             pltpu.VMEM((8, groups, taps), f32),
-            dma((5, PARTS)),
+            dma((3, PARTS)),
             dma((4, PARTS)),
             dma((7, PARTS)),
             dma((8, PARTS)),
+            dma((7, PARTS)),
+            dma((8, PARTS)),
+            dma((PARTS,)),
+            dma((PARTS,)),
             dma((2,)),
             dma((2,)),
             dma((8,)),

time: 85.2 us -> 85.2 us (level)
  no operation moved by 1% of the time
where the time goes in v2:
time: 85.2 us; the launch traced here: 85 us
  Pallas kernels  84.2 us (99%)
    pallas_call x1, Pallas kernels, fused_shards(): pl.pallas_call(functools.partial(mixer_kernel, group_size), out_shape=(pl...  82.5 us

profile of v2, /device:TPU:0, one launch (start us, length us, event | category | flops | bytes accessed | tf_op | source)
XLA Modules:
  0.0 85.0 jit_solution(15601899724649150304)
XLA Ops:
  0.6 82.5 %mixer.1 = (bf16[512,1024]{1,0:T(8,128)(2,1)S(1)}, bf16[512,1024]{1,0:T(8,128)(2,1)S(1)}, bf16[512,1024]{1,0:T(8,128)(2,1)S(1)}, f32[64,128]{1,0:T(8,128)S(1)}) custom-call(bf16[512,1024]{1,0:T(8,128)(2,1)} %cot_hbm.1, s32[1,512]{1,0:T(1,128)} %bitcast.1, f32[4]{0:T(128)} %class_ref.1, bf16[1024,512]{1,0:T(8,128)(2,1)} %w_ref.1, bf16[512,1024]{1,0:T(8,128)(2,1)} %q_hbm.1, ...), custom_call_target="tpu_custom_call" | custom-call | tf_op jit(solution)/shard_map/mixer/pallas_call | solution.py:693
  83.1 1.7 %store.1 = (bf16[512,1024]{1,0:T(8,128)(2,1)}, bf16[512,1024]{1,0:T(8,128)(2,1)}, bf16[512,1024]{1,0:T(8,128)(2,1)}, f32[64,128]{1,0:T(8,128)}) custom-call(bf16[512,1024]{1,0:T(8,128)(2,1)S(1)} %get-tuple-element.8.refs_0_, bf16[512,1024]{1,0:T(8,128)(2,1)S(1)} %get-tuple-element.9.refs_1_, bf16[512,1024]{1,0:T(8,128)(2,1)S(1)} %get-tuple-element.10.refs_2_, ...), custom_call_target="tpu_custom_call" | custom-call | tf_op jit(solution)/shard_map/store/pallas_call | solution.py:746

commit v3 on v2

--- a/solution.py
+++ b/solution.py
@@ -503,9 +503,7 @@
         for part in range(PARTS):
             wait_x(sd, part)
             x_copy(sd, sd, part, 6, sc, z).start()
-        relay_w(2)
         relay_wt(2)
-        relay_w(3)
         for part in range(PARTS):
             for slot in other:
                 wait_x(slot, part)
@@ -514,6 +512,7 @@
             wait_wt(far_end, part)
             partial_part(part)
             p_copy(part).start()
+            relay_w(part + 2)
         relay_wt(3)
 
     @pl.when(s > 0)
@@ -523,8 +522,21 @@
     forward_pair(0)
     forward_pair(1)
 
+    cross = 3 - s // 2
+    same = 1 - (cross // 2 + hi) % 2
+    late = same * cross + (1 - same) * far_mid
+    early_a = same * (cross + 1 - 2 * (cross % 2)) + (1 - same) * z
+    early_b = same * far_mid + (1 - same) * near
+
+    loads[4].wait()
+
     @pl.when(mid)
     def _():
+        for part in range(PARTS):
+            for slot in other[:3]:
+                wait_w(slot, part)
+        project(early_a, 0, rows, True)
+        project(early_b, 0, rows, False)
         relay_diagonal(0)
         relay_diagonal(2)
         wait_wt(far_end, 2)
@@ -536,8 +548,9 @@
         partial_part(3)
         p_copy(3).start()
         for part in range(PARTS):
-            for slot in other:
-                wait_w(slot, part)
+            wait_w(other[3], part)
+        project(late, 0, rows, False)
+        project(far_end, 0, rows, False)
 
     @pl.when(end_near)
     def _():
@@ -551,20 +564,12 @@
             for slot in other[2:]:
                 wait_w(slot, part)
 
-    loads[4].wait()
-    project(z, 0, rows, True)
-
     @pl.when(end)
     def _():
+        project(z, 0, rows, True)
         for part in range(PARTS):
             wait_wt(near, part)
-
-    project(near, 0, rows, False)
-
-    @pl.when(mid)
-    def _():
-        project(far_mid, 0, rows, False)
-        project(far_end, 0, rows, False)
+        project(near, 0, rows, False)
 
     loads[3].wait()
 

time: 85.2 us -> 83.1 us (0.975)
  Pallas kernels: 84.2 us -> 82.1 us
    pallas_call x1, Pallas kernels: 82.5 us -> 80.4 us  [fused_shards(): pl.pallas_call(functools.partial(mixer_kernel, group_size), out_shape=(pl...]
where the time goes in v3:
time: 83.1 us; the launch traced here: 82.9 us
  Pallas kernels  82.1 us (99%)
    pallas_call x1, Pallas kernels, fused_shards(): pl.pallas_call(functools.partial(mixer_kernel, group_size), out_shape=(pl...  80.4 us
    pallas_call x1, Pallas kernels, fused_shards(): pl.pallas_call(store_kernel, out_shape=tuple((jax.ShapeDtypeStruct(part.s...  1.7 us

profile of v3, /device:TPU:0, one launch (start us, length us, event | category | flops | bytes accessed | tf_op | source)
XLA Modules:
  0.0 82.9 jit_solution(9180345461343159063)
XLA Ops:
  0.6 80.4 %mixer.1 = (bf16[512,1024]{1,0:T(8,128)(2,1)S(1)}, bf16[512,1024]{1,0:T(8,128)(2,1)S(1)}, bf16[512,1024]{1,0:T(8,128)(2,1)S(1)}, f32[64,128]{1,0:T(8,128)S(1)}) custom-call(bf16[512,1024]{1,0:T(8,128)(2,1)} %cot_hbm.1, s32[1,512]{1,0:T(1,128)} %bitcast.1, f32[4]{0:T(128)} %class_ref.1, bf16[1024,512]{1,0:T(8,128)(2,1)} %w_ref.1, bf16[512,1024]{1,0:T(8,128)(2,1)} %q_hbm.1, ...), custom_call_target="tpu_custom_call" | custom-call | tf_op jit(solution)/shard_map/mixer/pallas_call | solution.py:698
  81.0 1.7 %store.1 = (bf16[512,1024]{1,0:T(8,128)(2,1)}, bf16[512,1024]{1,0:T(8,128)(2,1)}, bf16[512,1024]{1,0:T(8,128)(2,1)}, f32[64,128]{1,0:T(8,128)}) custom-call(bf16[512,1024]{1,0:T(8,128)(2,1)S(1)} %get-tuple-element.8.refs_0_, bf16[512,1024]{1,0:T(8,128)(2,1)S(1)} %get-tuple-element.9.refs_1_, bf16[512,1024]{1,0:T(8,128)(2,1)S(1)} %get-tuple-element.10.refs_2_, ...), custom_call_target="tpu_custom_call" | custom-call | tf_op jit(solution)/shard_map/store/pallas_call | solution.py:751
